TPU v7x, 256 devices: a whole 4x4x8 slice. The times are simulated.
256 devices in a mesh: row: 16 (over z, core), col: 8 (over x_hi, y), lrn: 2 (over x_lo).
Axes of the slice: x: 4 (x_hi: 2, x_lo: 2; x = x_hi * 2 + x_lo), y: 4, z: 8, core: 2. Of those that a mesh axis runs over, the one named last changes fastest.
Arguments:
- responses: int32 [4096, 16384], P('lrn', ('row', 'col')), may hold values 0 or 1
- observed: int32 [4096, 16384], P('lrn', ('row', 'col')), may hold values from 0 to 1, as said below
- qmatrix: int32 [16384, 8], P(('row', 'col')), may hold values from 0 to 1
- guess: float32 [16384], P(('row', 'col')), may hold values from 0.05 to 0.35
- slip: float32 [16384], P(('row', 'col')), may hold values from 0.05 to 0.35
Outputs:
- q3_scaled: float32 [16384, 16384], P('row', ('col', 'lrn'))
Inputs may be any that keep to these rules, and one draw needn't show every extreme that they name: Some items have no observed response from any learner.
All inputs are finite; a program needn't handle non-finite values. No bound on the sum of `responses` on one device may be relied on, other than what follows from the above.
Results may differ from a plain program's by a relative error of at most 0.008.
Values may be sent and summed in bfloat16 or wider, within the bound.
No kernel may reach another device: no remote copies, remote signals or barrier semaphores. Data moves between devices by JAX's collectives and lax.ppermute only.
A program may use at most 128 MiB of HBM per device.

v0:
```python
import jax
import jax.numpy as jnp
from jax import lax
from jax.sharding import PartitionSpec as P

ATTRS = 8
PROFILES = 256


def spread(x, axis, root):
    mine = lax.axis_index(axis) == root
    return lax.psum(jnp.where(mine, x, jnp.zeros_like(x)), axis)


def success(qmatrix, guess, slip):
    codes = jnp.arange(PROFILES, dtype=jnp.int32)
    powers = jnp.arange(ATTRS, dtype=jnp.int32)
    bits = (codes[None, :] >> powers[:, None] & 1).astype(jnp.float32)
    lacking = jnp.dot(qmatrix.astype(jnp.float32), 1.0 - bits, precision=lax.Precision.HIGHEST)
    return jnp.where(lacking == 0.0, 1.0 - slip[:, None], guess[:, None])


def learner_product(left, right):
    return lax.dot_general(
        left, right, (((0,), (0,)), ((), ())), preferred_element_type=jnp.float32
    )


def shards(responses, observed, qmatrix, guess, slip):
    prob = success(qmatrix, guess, slip)
    answered = responses.astype(jnp.float32)
    seen = observed.astype(jnp.float32)
    partial_value = jnp.dot(seen * answered, jnp.log(prob), precision=lax.Precision.HIGHEST)
    partial_value = partial_value + jnp.dot(
        seen * (1.0 - answered), jnp.log(1.0 - prob), precision=lax.Precision.HIGHEST
    )
    loglik = lax.psum(partial_value, ("row", "col"))
    posterior = jax.nn.softmax(loglik, axis=1).astype(jnp.bfloat16)
    expected = jnp.dot(posterior, prob.astype(jnp.bfloat16).T, preferred_element_type=jnp.float32)
    resid = seen * (answered - expected)
    count, total, square = lax.psum(
        (jnp.sum(seen, axis=0), jnp.sum(resid, axis=0), jnp.sum(resid * resid, axis=0)), "lrn"
    )
    count = jnp.maximum(count, 1.0)
    mean = total / count
    var = square / count - mean * mean
    zres = (seen * (resid - mean) * lax.rsqrt(var + 1e-06) * lax.rsqrt(count)).astype(jnp.bfloat16)
    panel = lax.all_gather(zres, "col", axis=1, tiled=True)
    learner_total = zres.shape[0] * lax.axis_size("lrn")
    whole_panel = lax.all_gather(panel, "lrn", axis=0, tiled=True)
    repeats = lax.axis_size("row") // (lax.axis_size("col") * lax.axis_size("lrn"))
    tile_index = lax.axis_index("col") * lax.axis_size("lrn") + lax.axis_index("lrn")
    pieces = spread(whole_panel, "row", tile_index * repeats + 0)
    gram = learner_product(whole_panel, pieces)
    return gram * jnp.sqrt(jnp.float32(learner_total))


def solution(mesh):
    placed = (
        P("lrn", ("row", "col")),
        P("lrn", ("row", "col")),
        P(("row", "col"), None),
        P(("row", "col")),
        P(("row", "col")),
    )
    return jax.shard_map(
        shards, mesh=mesh, in_specs=placed, out_specs=P("row", ("col", "lrn")), check_vma=False
    )
```

profile of v0, /device:TPU:2, one launch (start us, length us, event | category | flops | bytes accessed | tf_op | source)
XLA Modules:
  0.0 1652.2 jit_solution(6100974589586948307)
XLA Ops:
  6.5 0.0 copy-start
  6.5 0.0 copy-start.1
  6.5 0.0 all-reduce.4.cloned.1.call-start
  6.5 0.8 broadcast_subtract_fusion
  7.3 1.1 fusion
  8.4 0.0 copy-start.2
  8.5 3.4 fusion.3
  11.9 0.0 copy-done
  11.9 0.0 copy-done.1
  11.9 3.2 convolution_add_fusion
  15.1 0.0 copy-done.2
  15.1 0.0 all-reduce.4.cloned.1.call-update
  15.1 0.0 all-gather.3.cloned.1.call-start
  15.1 1279.9 %all-reduce.4.cloned.1.call-done = f32[2048,256]{1,0:T(8,128)} async-done(((f32[2048,256]{1,0:T(8,128)}), f32[2048,256]{1,0:T(8,128)}) %all-reduce.4.cloned.1.call-update) | async-done | bytes 2097168 | tf_op jit(solution)/shard_map/psum | solution.py:37
  1295.0 3.9 online-softmax
  1298.9 1.5 multiply_reduce_fusion
  1300.4 4.9 all-reduce
  1305.4 1.0 multiply_convert_fusion
  1306.4 0.0 all-gather.3.cloned.1.call-update
  1306.4 0.0 all-gather.5.cloned.1.call-start
  1306.5 72.4 %all-gather.3.cloned.1.call-done = bf16[2048,1024]{1,0:T(8,128)(2,1)} async-done(((bf16[2048,128]{1,0:T(8,128)(2,1)}), bf16[2048,1024]{1,0:T(8,128)(2,1)}) %all-gather.3.cloned.1.call-update) | async-done | bytes 4194320 | tf_op jit(solution)/shard_map/all_gather | solution.py:48
  1378.8 0.0 all-gather.5.cloned.1.call-update
  1378.9 0.0 all-reduce.6.cloned.1.call-start
  1378.9 108.7 %all-gather.5.cloned.1.call-done = bf16[4096,1024]{1,0:T(8,128)(2,1)} async-done(((bf16[2048,1024]{1,0:T(8,128)(2,1)}), bf16[4096,1024]{1,0:T(8,128)(2,1)}) %all-gather.5.cloned.1.call-update) | async-done | bytes 8388624 | tf_op jit(solution)/shard_map/all_gather | solution.py:50
  1487.6 3.8 broadcast_select_fusion
  1491.4 0.0 all-reduce.6.cloned.1.call-update
  1491.4 139.2 %all-reduce.6.cloned.1.call-done = bf16[4096,1024]{1,0:T(8,128)(2,1)} async-done(((bf16[4096,1024]{1,0:T(8,128)(2,1)}), bf16[4096,1024]{1,0:T(8,128)(2,1)}) %all-reduce.6.cloned.1.call-update) | async-done | bytes 8388624 | tf_op jit(solution)/shard_map/psum | solution.py:12
  1630.6 15.0 convolution_multiply_fusion
  (1 shorter events, 0.0 us)
Async XLA Ops:
  6.5 5.4 copy-start
  6.5 5.4 copy-start.1
  6.5 1288.5 %all-reduce.4.cloned.1.call-start = ((), (), s32[]{:S(2)}) async-start(), calls=%async_computation | async-start | bytes 4194304 | tf_op jit(solution)/shard_map/psum | solution.py:37
  8.4 6.6 copy-start.2
  15.1 1363.7 %all-gather.3.cloned.1.call-start = ((), (), s32[]{:S(2)}) async-start(), calls=%async_computation.1 | async-start | bytes 4718592 | tf_op jit(solution)/shard_map/all_gather | solution.py:48
  1306.4 181.2 %all-gather.5.cloned.1.call-start = ((), (), s32[]{:S(2)}) async-start(), calls=%async_computation.2 | async-start | bytes 12582912 | tf_op jit(solution)/shard_map/all_gather | solution.py:50
  1378.9 251.8 %all-reduce.6.cloned.1.call-start = ((), (), s32[]{:S(2)}) async-start(), calls=%async_computation.3 | async-start | bytes 16777216 | tf_op jit(solution)/shard_map/psum | solution.py:12
Sparse Core Ops, SparseCore 0:
  15.2 1279.7 all-reduce.3
  1306.5 72.2 all-gather.2
  1380.8 106.7 all-gather.4
  1491.5 139.0 all-reduce.5
where the time goes:
time: 1650 us
  waiting for transfers between devices  1600 us (97%)
  matrix products  22.7 us (1%)
    psum x1, waiting for transfers between devices, shards(): loglik = lax.psum(partial_value, ('row', 'col'))  1280 us
    psum x1, waiting for transfers between devices, spread(): return lax.psum(jnp.where(mine, x, jnp.zeros_like(x)), axis)  139 us
    all_gather x1, waiting for transfers between devices, shards(): whole_panel = lax.all_gather(panel, 'lrn', axis=0, tiled=True)  109 us
    all_gather x1, waiting for transfers between devices, shards(): panel = lax.all_gather(zres, 'col', axis=1, tiled=True)  72.4 us
  transfers between devices with their start and end apart: 4, of which 4 were waited for; matrix products, arithmetic and copies ran while one was open for 0% of the time, Pallas kernels for 0%

commit v1 on v0

--- a/solution.py
+++ b/solution.py
@@ -45,7 +45,9 @@
     mean = total / count
     var = square / count - mean * mean
     zres = (seen * (resid - mean) * lax.rsqrt(var + 1e-06) * lax.rsqrt(count)).astype(jnp.bfloat16)
-    panel = lax.all_gather(zres, "col", axis=1, tiled=True)
+    panel = jnp.concatenate(
+        lax.all_to_all(jnp.stack([zres for _ in range(lax.psum(1, "col"))], 0), "col", 0, 0), 1
+    )
     learner_total = zres.shape[0] * lax.axis_size("lrn")
     whole_panel = lax.all_gather(panel, "lrn", axis=0, tiled=True)
     repeats = lax.axis_size("row") // (lax.axis_size("col") * lax.axis_size("lrn"))

time: 1650 us -> 1620 us (0.982)
  waiting for transfers between devices: 1600 us -> 1520 us
  blocking collectives: 4.95 us -> 44.6 us
    all_gather x1 -> x0, waiting for transfers between devices: 72.4 us -> none  [shards(): panel = lax.all_gather(zres, 'col', axis=1, tiled=True)]
    all_to_all x0 -> x1, blocking collectives: none -> 39.5 us  [shards(): lax.all_to_all(jnp.stack([zres for _ in range(lax.psum(1, 'col'))], 0), '...]
  transfers between devices with their start and end apart: 4 -> 3, of which waited for: 4 -> 3; matrix products, arithmetic and copies ran while one was open for 0% -> 0% of each run, Pallas kernels for 0% -> 0%
where the time goes in v1:
time: 1620 us
  waiting for transfers between devices  1520 us (94%)
  blocking collectives  44.6 us (3%)
  matrix products  22.7 us (1%)
    psum x1, waiting for transfers between devices, shards(): loglik = lax.psum(partial_value, ('row', 'col'))  1280 us
    psum x1, waiting for transfers between devices, spread(): return lax.psum(jnp.where(mine, x, jnp.zeros_like(x)), axis)  139 us
    all_gather x1, waiting for transfers between devices, shards(): whole_panel = lax.all_gather(panel, 'lrn', axis=0, tiled=True)  105 us
    all_to_all x1, blocking collectives, shards(): lax.all_to_all(jnp.stack([zres for _ in range(lax.psum(1, 'col'))], 0), '...  39.5 us
  transfers between devices with their start and end apart: 3, of which 3 were waited for; matrix products, arithmetic and copies ran while one was open for 0% of the time, Pallas kernels for 0%

profile of v1, /device:TPU:2, one launch (start us, length us, event | category | flops | bytes accessed | tf_op | source)
XLA Modules:
  0.0 1616.1 jit_solution(8799988731505056821)
XLA Ops:
  6.5 0.0 copy-start
  6.5 0.0 copy-start.1
  6.5 0.0 all-reduce.4.cloned.1.call-start
  6.5 0.8 broadcast_subtract_fusion
  7.3 1.1 fusion
  8.4 0.0 copy-start.2
  8.5 3.4 fusion.3
  11.9 0.0 copy-done
  11.9 0.0 copy-done.1
  11.9 3.2 convolution_add_fusion
  15.1 0.0 copy-done.2
  15.1 0.0 all-reduce.4.cloned.1.call-update
  15.1 0.0 all-gather.2.cloned.1.call-start
  15.1 1279.9 %all-reduce.4.cloned.1.call-done = f32[2048,256]{1,0:T(8,128)} async-done(((f32[2048,256]{1,0:T(8,128)}), f32[2048,256]{1,0:T(8,128)}) %all-reduce.4.cloned.1.call-update) | async-done | bytes 2097168 | tf_op jit(solution)/shard_map/psum | solution.py:37
  1295.0 3.9 online-softmax
  1298.9 1.5 multiply_reduce_fusion
  1300.4 5.1 all-reduce
  1305.5 0.2 multiply_convert_fusion
  1305.7 0.2 copy.6
  1305.9 0.5 stack.2
  1306.5 39.5 %all_to_all.5 = bf16[8,2048,128]{1,2,0:T(8,128)(2,1)} all-to-all(bf16[8,2048,128]{1,2,0:T(8,128)(2,1)S(1)} %stack.2), channel_id=1, replica_groups=mesh['row'=16,'col'=8,'lrn'=2] {'col'}, dimensions={0} | all-to-all | bytes 8388608 | tf_op jit(solution)/shard_map/all_to_all | solution.py:49
  1346.0 0.0 all-gather.2.cloned.1.call-update
  1346.0 0.0 all-reduce.6.cloned.1.call-start
  1346.1 105.4 %all-gather.2.cloned.1.call-done = bf16[4096,1024]{0,1:T(8,128)(2,1)} async-done(((bf16[2048,1024]{0,1:T(8,128)(2,1)}), bf16[4096,1024]{0,1:T(8,128)(2,1)}) %all-gather.2.cloned.1.call-update) | async-done | bytes 8388624 | tf_op jit(solution)/shard_map/all_gather | solution.py:52
  1451.5 3.8 broadcast_select_fusion
  1455.2 0.0 all-reduce.6.cloned.1.call-update
  1455.3 139.2 %all-reduce.6.cloned.1.call-done = bf16[4096,1024]{0,1:T(8,128)(2,1)} async-done(((bf16[4096,1024]{0,1:T(8,128)(2,1)}), bf16[4096,1024]{0,1:T(8,128)(2,1)}) %all-reduce.6.cloned.1.call-update) | async-done | bytes 8388624 | tf_op jit(solution)/shard_map/psum | solution.py:12
  1594.5 15.0 convolution_multiply_fusion
  (1 shorter events, 0.0 us)
Async XLA Ops:
  6.5 5.4 copy-start
  6.5 5.4 copy-start.1
  6.5 1288.5 %all-reduce.4.cloned.1.call-start = ((), (), s32[]{:S(2)}) async-start(), calls=%async_computation.1 | async-start | bytes 4194304 | tf_op jit(solution)/shard_map/psum | solution.py:37
  8.4 6.6 copy-start.2
  15.1 1436.4 %all-gather.2.cloned.1.call-start = ((), (), s32[]{:S(2)}) async-start(), calls=%async_computation.2 | async-start | bytes 12582912 | tf_op jit(solution)/shard_map/all_gather | solution.py:52
  1346.0 248.5 %all-reduce.6.cloned.1.call-start = ((), (), s32[]{:S(2)}) async-start(), calls=%async_computation.3 | async-start | bytes 16777216 | tf_op jit(solution)/shard_map/psum | solution.py:12
Sparse Core Ops, SparseCore 0:
  15.2 1279.7 all-reduce.3
  1346.2 105.2 all-gather.1
  1455.4 139.0 all-reduce.5
